TPU v7x, 512 devices: a whole 4x4x16 slice. The times are simulated.
512 devices in a mesh: seq: 64 (over y, z), head: 8 (over x, core).
Axes of the slice: x: 4, y: 4, z: 16, core: 2. Of those that a mesh axis runs over, the one named last changes fastest.
Arguments:
- features: bfloat16 [32768, 2048], P('seq', 'head'), may hold values from -6 to 6
- gate_weight: bfloat16 [2048, 16], P('head'), may hold values from -0.125 to 0.125
- queries: bfloat16 [32768, 2048], P('seq', 'head'), may hold values from -6 to 6
- keys: bfloat16 [32768, 2048], P('seq', 'head'), may hold values from -40 to 40, as said below
- values: bfloat16 [32768, 2048], P('seq', 'head'), may hold values from -6 to 6
- log_decay: float32 [32768, 16], P('seq', 'head'), may hold values from -1.5 to 0, as said below
- ridge: float32 [16, 128], P('head'), may hold values from 0.02 to 0.5
Outputs:
- mixed: bfloat16 [32768, 2048], P('seq', 'head')
Inputs may be any that keep to these rules, and one draw needn't show every extreme that they name: `keys`: keys are real-valued of order one to ten in size. `log_decay`: each entry is at most zero.
All inputs are finite; a program needn't handle non-finite values.
Results may differ from a plain program's by a relative error of at most 0.001.
Values may be sent and summed in bfloat16 or wider, within the bound.
A program may use at most 64 MiB of HBM per device.

v0:
```python
import jax
import jax.numpy as jnp
from jax import lax
from jax.sharding import PartitionSpec as P

GROUP = 128
CG_STEPS = 4


HIGH = lax.Precision.HIGHEST


def carried_in(shard, axis, combine, identity):
    devices, place = (lax.axis_size(axis), lax.axis_index(axis))
    everything = jax.tree.map(lambda part: lax.all_gather(part, axis), shard)
    start = jax.tree.map(
        lambda part, zero: jnp.broadcast_to(jnp.asarray(zero, part.dtype), part.shape),
        shard,
        identity,
    )

    def turn(k, before):
        reached = k < place
        new = combine(before, jax.tree.map(lambda part: part[k], everything))
        return jax.tree.map(lambda a, b: jnp.where(reached, a, b), new, before)

    return lax.fori_loop(0, devices, turn, start)


def unit_rows(block):
    return block / jnp.sqrt(jnp.sum(block * block, axis=-1, keepdims=True) + 1e-06)


def join_three(earlier, later):
    factor = jnp.exp(later[0])[:, None, None]
    return (earlier[0] + later[0], factor * earlier[1] + later[1], factor * earlier[2] + later[2])


def body(features, gate_weight, queries, keys, values, log_decay, ridge):
    rows = queries.shape[0]
    heads = ridge.shape[0]
    width = ridge.shape[1]
    block_groups = rows // GROUP
    partial_logits = jnp.dot(features, gate_weight, preferred_element_type=jnp.float32)
    logits = lax.psum_scatter(partial_logits, "head", scatter_dimension=1, tiled=True)
    beta = jax.nn.sigmoid(logits).T.reshape(heads, block_groups, GROUP)
    decay = log_decay.T.reshape(heads, block_groups, GROUP)

    def separate_heads(arr):
        return (
            arr.astype(jnp.float32).reshape(block_groups, GROUP, heads, width).transpose(2, 0, 1, 3)
        )

    query_unit = unit_rows(separate_heads(queries))
    key_unit = unit_rows(separate_heads(keys))
    value_rows = separate_heads(values)
    within = jnp.cumsum(decay, axis=-1)
    lower = jnp.tril(jnp.ones((GROUP, GROUP), dtype=bool))
    spread = within[..., :, None] - within[..., None, :]
    weights = jnp.where(lower, jnp.exp(jnp.where(lower, spread, 0.0)), 0.0) * beta[..., None, :]
    lead = jnp.exp(within)[..., None]
    block_total = within[..., -1]
    factor = jnp.exp(block_total[..., None] - within) * beta
    upd_kk = jnp.einsum("hnci,hncj->hnij", key_unit * factor[..., None], key_unit, precision=HIGH)
    upd_vk = jnp.einsum("hnci,hncj->hnij", value_rows * factor[..., None], key_unit, precision=HIGH)

    def carry_step(carry, item):
        run_kk, run_vk = carry
        add_kk, add_vk, scale = item
        return ((scale * run_kk + add_kk, scale * run_vk + add_vk), (run_kk, run_vk))

    zero_state = jnp.zeros((heads, width, width), jnp.float32)
    items = (
        jnp.moveaxis(upd_kk, 1, 0),
        jnp.moveaxis(upd_vk, 1, 0),
        jnp.exp(block_total).T[:, :, None, None],
    )
    totals, local_starts = lax.scan(carry_step, (zero_state, zero_state), items)
    local_kk = jnp.moveaxis(local_starts[0], 0, 1)
    local_vk = jnp.moveaxis(local_starts[1], 0, 1)
    device_decay = jnp.sum(block_total, axis=-1)
    reach = jnp.exp(jnp.cumsum(block_total, axis=-1) - block_total)[..., None, None]
    zero_decay = jnp.zeros((heads,), jnp.float32)
    incoming = carried_in(
        (device_decay, totals[0], totals[1]),
        "seq",
        join_three,
        (zero_decay, zero_state, zero_state),
    )
    start_kk = local_kk + reach * incoming[1][:, None]
    start_vk = local_vk + reach * incoming[2][:, None]
    ridge_wide = ridge[:, None, None, :]
    solution = jnp.zeros_like(query_unit)
    resid = query_unit
    direction = query_unit
    norm_now = jnp.sum(resid * resid, axis=-1, keepdims=True)
    for step in range(CG_STEPS):
        inner = jnp.einsum("hncj,hnij->hnci", direction, start_kk, precision=HIGH)
        apply_scores = jnp.einsum("hncj,hntj->hnct", direction, key_unit, precision=HIGH) * weights
        image = (
            lead * inner
            + jnp.einsum("hnct,hntj->hncj", apply_scores, key_unit, precision=HIGH)
            + ridge_wide * direction
        )
        alpha = norm_now / jnp.sum(direction * image, axis=-1, keepdims=True)
        solution = solution + alpha * direction
        resid = resid - alpha * image
        norm_next = jnp.sum(resid * resid, axis=-1, keepdims=True)
        direction = resid + norm_next / norm_now * direction
        norm_now = norm_next
    scores = jnp.einsum("hncj,hntj->hnct", solution, key_unit, precision=HIGH) * weights
    readout = lead * jnp.einsum("hncj,hnij->hnci", solution, start_vk, precision=HIGH)
    readout = readout + jnp.einsum("hnct,hntj->hncj", scores, value_rows, precision=HIGH)
    return readout.transpose(1, 2, 0, 3).reshape(rows, heads * width).astype(jnp.bfloat16)


def solution(mesh):
    placed = (
        P("seq", "head"),
        P("head", None),
        P("seq", "head"),
        P("seq", "head"),
        P("seq", "head"),
        P("seq", "head"),
        P("head", None),
    )
    return jax.shard_map(
        body, mesh=mesh, in_specs=placed, out_specs=P("seq", "head"), check_vma=False
    )
```

profile of v0, /device:TPU:24, one launch (start us, length us, event | category | flops | bytes accessed | tf_op | source)
XLA Modules:
  0.0 454.6 jit_solution(7709055330159902065)
XLA Ops:
  6.5 1.2 reshape.120
  8.0 1.2 reshape.119
  11.8 25.6 %all-reduce.1 = f32[512,16]{0,1:T(8,128)S(1)} all-reduce(f32[512,16]{0,1:T(8,128)S(1)} %fusion.34), channel_id=5, replica_groups=mesh['seq'=64,'head'=8] {'head'}, use_global_device_ids=true, to_apply=%region_4.5.clone | all-reduce | flops 8192 | bytes 65536
  37.5 1.3 dynamic-slice.1
  40.7 1.8 convolution_bitcast_fusion.3
  42.5 1.3 convolution_bitcast_fusion.2
  44.0 3.2 while.33
  48.6 1.3 dynamic-slice
  50.8 129.1 %all-reduce = f32[128]{0:T(128)S(1)} all-reduce(f32[128]{0:T(128)S(1)} %dynamic-update-slice), channel_id=2, replica_groups=mesh['seq'=64,'head'=8] {'seq'}, use_global_device_ids=true, to_apply=%add | all-reduce | flops 128 | bytes 1024
  180.2 2.1 convolution_multiply_fusion.7
  182.2 21.7 %all-gather.6.cloned.1.call-done = f32[128,128,128]{2,1,0:T(8,128)} async-done(((f32[2,128,128]{2,1,0:T(8,128)}), f32[128,128,128]{2,1,0:T(8,128)}) %all-gather.6.cloned.1.call-update) | async-done | bytes 8388624 | tf_op jit(solution)/shard_map/all_gather | solution.py:15
  204.0 154.1 %all-gather.8.cloned.1.call-done = f32[128,128,128]{2,1,0:T(8,128)} async-done(((f32[2,128,128]{2,1,0:T(8,128)}), f32[128,128,128]{2,1,0:T(8,128)}) %all-gather.8.cloned.1.call-update) | async-done | bytes 8388624 | tf_op jit(solution)/shard_map/all_gather | solution.py:15
  358.1 71.4 %while.34 = (s32[]{:T(128)}, f32[2,128,128]{2,1,0:T(8,128)S(1)}, f32[2,128,128]{2,1,0:T(8,128)S(1)}, s32[]{:T(128)}, f32[64,2]{1,0:T(8,128)S(1)}, /*index=5*/f32...) while((s32[]{:T(128)}, f32[2,128,128]{2,1,0:T(8,128)S(1)}, ...), condition=%wide.region_10.11_spmd.clone, body=%wide.region_9.10_spmd.clone.sunk | while | flops 262148 | bytes 786577 | solution.py:27
  359.2 1.1 fusion.55
  360.3 1.1 fusion.55
  361.4 1.1 fusion.55
  362.5 1.1 fusion.55
  363.6 1.1 fusion.55
  364.7 1.1 fusion.55
  367.0 1.1 fusion.55
  368.1 1.1 fusion.55
  369.2 1.1 fusion.55
  372.5 1.1 fusion.55
  373.7 1.1 fusion.55
  374.8 1.1 fusion.55
  378.1 1.1 fusion.55
  379.2 1.1 fusion.55
  380.3 1.1 fusion.55
  382.6 1.1 fusion.55
  383.7 1.1 fusion.55
  384.8 1.1 fusion.55
  388.1 1.1 fusion.55
  389.2 1.1 fusion.55
  390.4 1.1 fusion.55
  393.7 1.1 fusion.55
  394.8 1.1 fusion.55
  395.9 1.1 fusion.55
  399.3 1.1 fusion.55
  400.4 1.1 fusion.55
  401.5 1.1 fusion.55
  403.7 1.1 fusion.55
  404.8 1.1 fusion.55
  406.0 1.1 fusion.55
  409.3 1.1 fusion.55
  410.4 1.1 fusion.55
  411.5 1.1 fusion.55
  414.9 1.1 fusion.55
  416.0 1.1 fusion.55
  417.1 1.1 fusion.55
  420.4 1.1 fusion.55
  421.5 1.1 fusion.55
  422.7 1.1 fusion.55
  424.9 1.1 fusion.55
  426.0 1.1 fusion.55
  427.1 1.1 fusion.55
  430.4 2.3 multiply_reduce_fusion.5
  433.0 1.4 convolution_multiply_fusion.5
  435.0 1.3 multiply_reduce_fusion.3
  436.5 1.4 convolution_multiply_fusion.3
  438.6 1.3 multiply_reduce_fusion.1
  440.1 1.4 convolution_multiply_fusion.1
  442.1 1.3 fusion.13
  443.6 1.6 convolution_multiply_fusion
  445.6 1.1 fusion.12
  (160 shorter events, 38.6 us)
Async XLA Ops:
  6.5 4.4 copy-start
  6.5 197.4 %all-gather.6.cloned.1.call-start = ((), (), s32[]{:S(2)}) async-start(), calls=%async_computation | async-start | bytes 8519680 | tf_op jit(solution)/shard_map/all_gather | solution.py:15
  47.1 0.7 copy-start.1
  47.1 0.7 copy-start.2
  47.2 382.3 %copy-start.3 = (f32[4,2,128,128]{3,2,1,0:T(8,128)S(1)}, f32[4,2,128,128]{3,2,1,0:T(8,128)}, u32[]{:S(2)}) copy-start(f32[4,2,128,128]{3,2,1,0:T(8,128)} %get-tuple-element.179) | copy-start | bytes 1572868
  47.2 383.2 %copy-start.4 = (f32[2,128]{1,0:T(2,128)S(1)}, f32[2,128]{1,0:T(2,128)}, u32[]{:S(2)}) copy-start(f32[2,128]{1,0:T(2,128)} %param.17) | copy-start | bytes 3076
  47.8 310.2 %all-gather.8.cloned.1.call-start = ((), (), s32[]{:S(2)}) async-start(), calls=%async_computation.1 | async-start | bytes 8519680 | tf_op jit(solution)/shard_map/all_gather | solution.py:15
Sparse Core Ops, SparseCore 0:
  47.9 155.9 all-gather.5
  206.9 151.0 all-gather.7
where the time goes:
time: 458 us; the launch traced here: 455 us
  waiting for transfers between devices  177 us (39%)
  blocking collectives  155 us (34%)
  other arithmetic  74.1 us (16%)
  matrix products  22 us (5%)
  between operations  15 us (3%)
  local copies, waits for them, and re-layouts  9.91 us (2%)
    all_gather x2, waiting for transfers between devices, carried_in(): everything = jax.tree.map(lambda part: lax.all_gather(part, axis), shard)  176 us
    unnamed x2, blocking collectives  155 us
    select_n x64, other arithmetic, turn(): return jax.tree.map(lambda a, b: jnp.where(reached, a, b), new, before)  68.5 us
  transfers between devices with their start and end apart: 2, of which 2 were waited for; matrix products, arithmetic and copies ran while one was open for 1% of the time, Pallas kernels for 0%

commit v1 on v0

v1 whole, which is shorter than its diff:
```python
import functools

import jax
import jax.numpy as jnp
from jax import lax
from jax.experimental import pallas as pl
from jax.experimental.pallas import tpu as pltpu
from jax.sharding import PartitionSpec as P

CG_STEPS = 4
BLOCK = 256
MESH = pl.DeviceIdType.MESH
F32 = jnp.float32
BF16 = jnp.bfloat16


def nn(a, b):
    return jnp.dot(a, b, preferred_element_type=F32)


def nt(a, b):
    return lax.dot_general(a, b, (((1,), (1,)), ((), ())), preferred_element_type=F32)


def tn(a, b):
    return lax.dot_general(a, b, (((0,), (0,)), ((), ())), preferred_element_type=F32)


def split(a):
    hi = a.astype(BF16)
    return hi, (a - hi.astype(F32)).astype(BF16)


def column_sums(sq):
    ones = jnp.ones((8, sq.shape[1]), BF16)
    hi, lo = split(sq)
    return nt(ones, hi) + nt(ones, lo)


def kernel(
    ny, nz, nh, feat, gw, q_ref, k_ref, v_ref, ld_ref, ridge_ref, out_ref,
    gsend, grecv, sbuf, rbuf, ybuf, yrecv, tbuf, trecv, w1_ref, w2_ref, s1_ref, in1_ref,
    gs_sem, gr_sem, ss_sem, sr_sem, ys_sem, yr_sem, ts_sem, tr_sem,
):
    rows = q_ref.shape[0]
    heads = ridge_ref.shape[0]
    width = ridge_ref.shape[1]
    blocks = rows // BLOCK
    part = width // nz
    seq = lax.axis_index("seq")
    me_h = lax.axis_index("head")
    me_y = seq // nz
    me_z = seq % nz

    barrier = pltpu.get_barrier_semaphore()
    for d in range(1, nh):
        pl.semaphore_signal(barrier, inc=1, device_id={"head": (me_h + d) % nh}, device_id_type=MESH)
    order = sorted(range(1, nz), key=lambda d: -min(d, nz - d))
    for d in order:
        pl.semaphore_signal(
            barrier, inc=1, device_id={"seq": me_y * nz + (me_z + d) % nz}, device_id_type=MESH
        )
    for d in range(1, ny):
        pl.semaphore_signal(
            barrier, inc=1, device_id={"seq": ((me_y + d) % ny) * nz + me_z}, device_id_type=MESH
        )

    partial = nt(gw[...], feat[...])
    for j in range(nh):
        gsend[j] = partial[heads * j : heads * (j + 1)]

    pl.semaphore_wait(barrier, nh - 1 + nz - 1 + ny - 1)

    gate_copies = []
    for d in range(1, nh):
        to = (me_h + d) % nh
        c = pltpu.make_async_remote_copy(
            src_ref=gsend.at[to], dst_ref=grecv.at[me_h], send_sem=gs_sem.at[d],
            recv_sem=gr_sem.at[d], device_id={"head": to}, device_id_type=MESH,
        )
        c.start()
        gate_copies.append(c)
    grecv[me_h] = gsend[me_h]

    within = jnp.concatenate([ld_ref[...]] * (8 // heads), axis=0)
    place = lax.broadcasted_iota(jnp.int32, (8, rows), 1) % BLOCK
    step = 1
    while step < BLOCK:
        within = within + jnp.where(place >= step, pltpu.roll(within, step, 1), 0.0)
        step *= 2
    ksq = []
    for h in range(heads):
        kf = k_ref[:, h * width : (h + 1) * width].astype(F32)
        ksq.append(column_sums(kf * kf)[0:1])
    knorm = jnp.sqrt(jnp.concatenate(ksq, axis=0) + 1e-06)
    kinv = 1.0 / knorm
    within = within[0:heads]
    ends = [within[:, (b + 1) * BLOCK - 1 : (b + 1) * BLOCK] for b in range(blocks)]
    total_row = jnp.concatenate([jnp.broadcast_to(e, (heads, BLOCK)) for e in ends], axis=1)
    tail = jnp.exp(total_row - within)
    ltot = functools.reduce(lambda a, b: a + b, ends)

    qunit, qinv = [], []
    for h in range(heads):
        qf = q_ref[:, h * width : (h + 1) * width].astype(F32)
        root = jnp.sqrt(jnp.sum(qf * qf, axis=-1, keepdims=True) + 1e-06)
        qunit.append(qf / root)
        qinv.append(1.0 / root)

    for c in gate_copies:
        c.wait()
    logits = grecv[0]
    for j in range(1, nh):
        logits = logits + grecv[j]
    beta = 1.0 / (1.0 + jnp.exp(-logits))
    vfac = tail * beta * kinv
    kfac = vfac * kinv
    rows8 = jnp.concatenate([kfac, vfac, within, jnp.exp(within)], axis=0)
    cols = jnp.transpose(jnp.concatenate([rows8] * (128 // rows8.shape[0]), axis=0))

    def col(kind, h, b):
        return cols[b * BLOCK : (b + 1) * BLOCK, kind * heads + h : kind * heads + h + 1]

    def keys(h, b):
        return k_ref[b * BLOCK : (b + 1) * BLOCK, h * width : (h + 1) * width]

    def values(h, b):
        return v_ref[b * BLOCK : (b + 1) * BLOCK, h * width : (h + 1) * width]

    updates = []
    for h in range(heads):
        ups = []
        for b in range(blocks):
            kb = keys(h, b)
            fk = kb.astype(F32) * col(0, h, b)
            fv = values(h, b).astype(F32) * col(1, h, b)
            hi, lo = split(jnp.concatenate([fk, fv], axis=1))
            ups.append(tn(kb, hi) + tn(kb, lo))
        updates.append(ups)
        total = ups[0]
        for b in range(1, blocks):
            total = total * jnp.exp(ends[b][h : h + 1]) + ups[b]
        for c in range(nz):
            sbuf[h, c, 0:part] = total[c * part : (c + 1) * part, 0:width]
            sbuf[h, c, part : 2 * part] = total[c * part : (c + 1) * part, width:]
            sbuf[h, c, 2 * part : 2 * part + 1] = jnp.broadcast_to(ltot[h : h + 1], (1, width))

    msg = 2 * part + 1
    sends = []
    for h in range(heads):
        for d in order:
            to = (me_z + d) % nz
            c = pltpu.make_async_remote_copy(
                src_ref=sbuf.at[h, to, pl.ds(0, msg)], dst_ref=rbuf.at[h, me_z, pl.ds(0, msg)],
                send_sem=ss_sem.at[h, d], recv_sem=sr_sem.at[h, d],
                device_id={"seq": me_y * nz + to}, device_id_type=MESH,
            )
            c.start()
            sends.append(c)
        rbuf[h, me_z] = sbuf[h, me_z]

    lower = lax.broadcasted_iota(jnp.int32, (BLOCK, BLOCK), 0) >= lax.broadcasted_iota(
        jnp.int32, (BLOCK, BLOCK), 1
    )
    row1 = beta * kinv * kinv
    row2 = beta * kinv
    for h in range(heads):
        for b in range(blocks):
            i = h * blocks + b
            sl = slice(b * BLOCK, (b + 1) * BLOCK)
            spread = col(2, h, b) - within[h : h + 1, sl]
            decay = jnp.where(lower, jnp.exp(jnp.minimum(spread, 0.0)), 0.0)
            w1 = decay * row1[h : h + 1, sl]
            w1_ref[i] = w1
            w2_ref[i] = decay * row2[h : h + 1, sl]
            kb = keys(h, b)
            s = nt(q_ref[sl, h * width : (h + 1) * width], kb) * qinv[h][sl]
            s1_ref[i] = s
            hi, lo = split(s * w1)
            in1_ref[i] = nn(hi, kb) + nn(lo, kb)

    y_copies = []
    for h in range(heads):
        for d in range(1, nz):
            sends[h * (nz - 1) + d - 1].wait()
        state = jnp.zeros((2 * part, width), F32)
        reach = jnp.zeros((1, width), F32)
        for z in range(nz):
            tbuf[h, z, 0 : 2 * part] = state
            tbuf[h, z, 2 * part : 2 * part + 1] = reach
            log = rbuf[h, z, 2 * part : 2 * part + 1]
            state = jnp.exp(log) * state + rbuf[h, z, 0 : 2 * part]
            reach = reach + log
        ybuf[h, 0 : 2 * part] = state
        ybuf[h, 2 * part : 2 * part + 1] = reach
        yrecv[h, me_y] = ybuf[h]
        for d in range(1, ny):
            to = (me_y + d) % ny
            c = pltpu.make_async_remote_copy(
                src_ref=ybuf.at[h, pl.ds(0, msg)], dst_ref=yrecv.at[h, me_y, pl.ds(0, msg)],
                send_sem=ys_sem.at[h, d], recv_sem=yr_sem.at[h, d],
                device_id={"seq": to * nz + me_z}, device_id_type=MESH,
            )
            c.start()
            y_copies.append(c)

    returns = []
    for h in range(heads):
        for d in range(1, ny):
            y_copies[h * (ny - 1) + d - 1].wait()
        carry = jnp.zeros((2 * part, width), F32)
        for y in range(ny):
            new = jnp.exp(yrecv[h, y, 2 * part : 2 * part + 1]) * carry + yrecv[h, y, 0 : 2 * part]
            carry = jnp.where(y < me_y, new, carry)
        for z in range(nz):
            tbuf[h, z, 0 : 2 * part] = (
                tbuf[h, z, 0 : 2 * part] + jnp.exp(tbuf[h, z, 2 * part : 2 * part + 1]) * carry
            )
        for d in order:
            to = (me_z + d) % nz
            c = pltpu.make_async_remote_copy(
                src_ref=tbuf.at[h, to, pl.ds(0, 2 * part)],
                dst_ref=trecv.at[h, me_z, pl.ds(0, 2 * part)],
                send_sem=ts_sem.at[h, d], recv_sem=tr_sem.at[h, d],
                device_id={"seq": me_y * nz + to}, device_id_type=MESH,
            )
            c.start()
            returns.append(c)
        trecv[h, me_z] = tbuf[h, me_z, 0 : 2 * part]

    for h in range(heads):
        for d in range(1, nz):
            returns[h * (nz - 1) + d - 1].wait()
        start = jnp.concatenate(
            [
                trecv[h, :, 0:part].reshape(width, width),
                trecv[h, :, part : 2 * part].reshape(width, width),
            ],
            axis=1,
        )
        ridge = ridge_ref[h : h + 1]
        for b in range(blocks):
            i = h * blocks + b
            sl = slice(b * BLOCK, (b + 1) * BLOCK)
            if b > 0:
                start = start * jnp.exp(ends[b - 1][h : h + 1]) + updates[h][b - 1]
            hi, lo = split(start)
            khi, klo, vhi, vlo = hi[:, :width], lo[:, :width], hi[:, width:], lo[:, width:]
            zero = jnp.zeros_like(klo)
            kk_pair = jnp.concatenate(
                [jnp.concatenate([khi, klo], axis=1), jnp.concatenate([khi, zero], axis=1)], axis=0
            )
            vk_pair = jnp.concatenate(
                [jnp.concatenate([vhi, vlo], axis=1), jnp.concatenate([vhi, zero], axis=1)], axis=0
            )
            kb = keys(h, b)
            vb = values(h, b)
            k_wide = jnp.concatenate([kb, kb], axis=1)
            k_tall = jnp.concatenate([kb, kb], axis=0)
            v_tall = jnp.concatenate([vb, vb], axis=0)
            lead = col(3, h, b)
            w1 = w1_ref[i]
            p = qunit[h][sl]
            r = p
            norm = jnp.sum(r * r, axis=-1, keepdims=True)
            s = s1_ref[i]
            both = nn(q_ref[sl, h * width : (h + 1) * width], kk_pair[:width])
            state_part = (both[:, :width] + both[:, width:]) * (lead * qinv[h][sl])
            x = jnp.zeros_like(p)
            s_sum = jnp.zeros_like(s)
            for step in range(CG_STEPS):
                if step > 0:
                    ph, plo = split(p)
                    pair = jnp.concatenate([ph, plo], axis=1)
                    both = nn(pair, kk_pair)
                    state_part = lead * (both[:, :width] + both[:, width:])
                    s = nt(pair, k_wide)
                near = state_part + ridge * p
                sw = s * w1
                if step == CG_STEPS - 1:
                    energy = jnp.sum(p * near, axis=-1, keepdims=True) + jnp.sum(
                        s * sw, axis=-1, keepdims=True
                    )
                    alpha = norm / energy
                    x = x + alpha * p
                    s_sum = s_sum + alpha * s
                    break
                if step == 0:
                    image = near + in1_ref[i]
                else:
                    sh, slo = split(sw)
                    image = near + nn(jnp.concatenate([sh, slo], axis=1), k_tall)
                alpha = norm / jnp.sum(p * image, axis=-1, keepdims=True)
                x = x + alpha * p
                s_sum = s_sum + alpha * s
                r = r - alpha * image
                after = jnp.sum(r * r, axis=-1, keepdims=True)
                p = r + (after / norm) * p
                norm = after
            xh, xlo = split(x)
            both = nn(jnp.concatenate([xh, xlo], axis=1), vk_pair)
            sh, slo = split(s_sum * w2_ref[i])
            mixed = lead * (both[:, :width] + both[:, width:]) + nn(
                jnp.concatenate([sh, slo], axis=1), v_tall
            )
            out_ref[sl, h * width : (h + 1) * width] = mixed.astype(BF16)


def body(ny, nz, nh, features, gate_weight, queries, keys, values, log_decay, ridge):
    rows = queries.shape[0]
    heads, width = ridge.shape
    blocks = rows // BLOCK
    part = width // nz
    vmem = pl.BlockSpec(memory_space=pltpu.VMEM)
    pad = -(-(2 * part + 1) // 8) * 8
    dma = pltpu.SemaphoreType.DMA
    return pl.pallas_call(
        functools.partial(kernel, ny, nz, nh),
        out_shape=jax.ShapeDtypeStruct((rows, heads * width), BF16),
        in_specs=[vmem] * 7,
        out_specs=vmem,
        scratch_shapes=[
            pltpu.VMEM((nh, heads, rows), F32),
            pltpu.VMEM((nh, heads, rows), F32),
            pltpu.VMEM((heads, nz, pad, width), F32),
            pltpu.VMEM((heads, nz, pad, width), F32),
            pltpu.VMEM((heads, pad, width), F32),
            pltpu.VMEM((heads, ny, pad, width), F32),
            pltpu.VMEM((heads, nz, pad, width), F32),
            pltpu.VMEM((heads, nz, 2 * part, width), F32),
            pltpu.VMEM((heads * blocks, BLOCK, BLOCK), F32),
            pltpu.VMEM((heads * blocks, BLOCK, BLOCK), F32),
            pltpu.VMEM((heads * blocks, BLOCK, BLOCK), F32),
            pltpu.VMEM((heads * blocks, BLOCK, width), F32),
            dma((nh,)), dma((nh,)), dma((heads, nz)), dma((heads, nz)),
            dma((heads, ny)), dma((heads, ny)), dma((heads, nz)), dma((heads, nz)),
        ],
        compiler_params=pltpu.CompilerParams(collective_id=0, has_side_effects=True),
        name="mesa",
    )(features, gate_weight.T, queries, keys, values, log_decay.T, ridge)


def solution(mesh):
    seq, nh = mesh.shape["seq"], mesh.shape["head"]
    nz = 16 if seq >= 64 else seq // 2
    placed = (
        P("seq", "head"),
        P("head", None),
        P("seq", "head"),
        P("seq", "head"),
        P("seq", "head"),
        P("seq", "head"),
        P("head", None),
    )
    return jax.shard_map(
        functools.partial(body, seq // nz, nz, nh),
        mesh=mesh, in_specs=placed, out_specs=P("seq", "head"), check_vma=False,
    )
```

time: 458 us -> 57.1 us (0.12)
  waiting for transfers between devices: 177 us -> 0 us
  blocking collectives: 155 us -> 0 us
  other arithmetic: 74.1 us -> 0 us
  Pallas kernels: 0 us -> 55.1 us
  matrix products: 22 us -> 0 us
  between operations: 15 us -> 0.01 us
  local copies, waits for them, and re-layouts: 9.91 us -> 1.67 us
    all_gather x2 -> x0, waiting for transfers between devices: 176 us -> none  [carried_in(): everything = jax.tree.map(lambda part: lax.all_gather(part, axis), shard)]
    unnamed x2 -> x0, blocking collectives: 155 us -> none
    select_n x64 -> x0, other arithmetic: 68.5 us -> none  [turn(): return jax.tree.map(lambda a, b: jnp.where(reached, a, b), new, before)]
    pallas_call x0 -> x1, Pallas kernels: none -> 55.1 us  [body(): pl.pallas_call(functools.partial(kernel, ny, nz, nh), out_shape=jax.Shape...]
    dot_general x18 -> x0, matrix products: 22 us -> none  [the longest x4 6.2 us: body(): jnp.einsum('hncj,hntj->hnct', direction, key_unit, precision=HIGH) * weights]
  transfers between devices with their start and end apart: 2 -> 0, of which waited for: 2 -> 0; matrix products, arithmetic and copies ran while one was open for 1% -> 0% of each run, Pallas kernels for 0% -> 0%
where the time goes in v1:
time: 57.1 us; the launch traced here: 56.8 us
  Pallas kernels  55.1 us (96%)
  local copies, waits for them, and re-layouts  1.67 us (3%)
    pallas_call x1, Pallas kernels, body(): pl.pallas_call(functools.partial(kernel, ny, nz, nh), out_shape=jax.Shape...  55.1 us
    unnamed x1, local copies, waits for them, and re-layouts  1.67 us

profile of v1, /device:TPU:24, one launch (start us, length us, event | category | flops | bytes accessed | tf_op | source)
XLA Modules:
  0.0 56.8 jit_solution(7059313967771379346)
XLA Ops:
  0.0 55.1 %mesa.1 = bf16[512,256]{1,0:T(8,128)(2,1)} custom-call(bf16[512,256]{1,0:T(8,128)(2,1)} %feat.1, bf16[16,256]{1,0:T(8,128)(2,1)} %bitcast.2, bf16[512,256]{1,0:T(8,128)(2,1)} %q_ref.1, bf16[512,256]{1,0:T(8,128)(2,1)} %k_ref.1, bf16[512,256]{1,0:T(8,128)(2,1)} %v_ref.1, f32[2,512]{1,0:T(2,128)} %bitcast.3, f32[2,128]{1,0:T(2,128)} %ridge_ref.1), custom_call_target="tpu_custom_call" | custom-call | tf_op jit(solution)/shard_map/mesa/pallas_call | solution.py:317
  55.1 1.7 %copy.9 = bf16[512,256]{1,0:T(8,128)(2,1)} copy(bf16[512,256]{1,0:T(8,128)(2,1)} %mesa.1) | data formatting | bytes 524288

commit v2 on v1

--- a/solution.py
+++ b/solution.py
@@ -37,57 +37,107 @@
     return nt(ones, hi) + nt(ones, lo)
 
 
+def pack(total, width):
+    half = width // 2
+    lane = lax.broadcasted_iota(jnp.int32, (half, width), 1)
+    row = lax.broadcasted_iota(jnp.int32, (half, width), 0)
+    top = total[0:half, 0:width]
+    turned = pltpu.roll(total[half:width, 0:width], half, 1)
+    folded = jnp.where(lane >= row, top, turned)
+    diagonal = jnp.sum(jnp.where(lane == row, turned, 0.0), axis=0, keepdims=True)
+    return total[:, width:], folded, diagonal
+
+
+def unpack(vkt, folded, diagonal, width):
+    half = width // 2
+    lane = lax.broadcasted_iota(jnp.int32, (half, width), 1)
+    row = lax.broadcasted_iota(jnp.int32, (half, width), 0)
+    flipped = jnp.transpose(jnp.concatenate([folded, jnp.zeros_like(folded)], axis=0))
+    top = jnp.where(lane >= row, folded, flipped[0:half])
+    corner = jnp.where(lane == row, diagonal, jnp.where(lane < row, folded, flipped[0:half]))
+    bottom = jnp.where(lane < half, flipped[half:width], pltpu.roll(corner, half, 1))
+    return jnp.concatenate([jnp.concatenate([top, bottom], axis=0), vkt], axis=1)
+
+
 def kernel(
-    ny, nz, nh, feat, gw, q_ref, k_ref, v_ref, ld_ref, ridge_ref, out_ref,
+    ny, nz, nh, feat_hbm, gw_hbm, q_hbm, k_hbm, v_hbm, ld_hbm, ridge_hbm, out_ref,
+    feat, gw, q_ref, k_ref, v_ref, ld_ref, ridge_ref,
     gsend, grecv, sbuf, rbuf, ybuf, yrecv, tbuf, trecv, w1_ref, w2_ref, s1_ref, in1_ref,
-    gs_sem, gr_sem, ss_sem, sr_sem, ys_sem, yr_sem, ts_sem, tr_sem,
+    in_sem, ready, gs_sem, gr_sem, ss_sem, sr_sem, ys_sem, yr_sem, ts_sem, tr_sem,
 ):
     rows = q_ref.shape[0]
     heads = ridge_ref.shape[0]
     width = ridge_ref.shape[1]
     blocks = rows // BLOCK
     part = width // nz
+    fold = part // 2
+    body_rows = part + fold + 1
     seq = lax.axis_index("seq")
     me_h = lax.axis_index("head")
     me_y = seq // nz
     me_z = seq % nz
 
+    def at_z(d):
+        return {"seq": me_y * nz + (me_z + d + nz) % nz}
+
+    def at_y(d):
+        return {"seq": ((me_y + d) % ny) * nz + me_z}
+
+    def signal(sem, where):
+        pl.semaphore_signal(sem, inc=1, device_id=where, device_id_type=MESH)
+
+    def send(src, dst, sem_out, sem_in, where):
+        c = pltpu.make_async_remote_copy(
+            src_ref=src, dst_ref=dst, send_sem=sem_out, recv_sem=sem_in,
+            device_id=where, device_id_type=MESH,
+        )
+        c.start()
+        return c
+
     barrier = pltpu.get_barrier_semaphore()
     for d in range(1, nh):
-        pl.semaphore_signal(barrier, inc=1, device_id={"head": (me_h + d) % nh}, device_id_type=MESH)
-    order = sorted(range(1, nz), key=lambda d: -min(d, nz - d))
-    for d in order:
-        pl.semaphore_signal(
-            barrier, inc=1, device_id={"seq": me_y * nz + (me_z + d) % nz}, device_id_type=MESH
-        )
+        signal(barrier, {"head": (me_h + d) % nh})
+    for d in (1, -1):
+        signal(barrier, at_z(d))
     for d in range(1, ny):
-        pl.semaphore_signal(
-            barrier, inc=1, device_id={"seq": ((me_y + d) % ny) * nz + me_z}, device_id_type=MESH
-        )
-
+        signal(barrier, at_y(d))
+
+    loads = []
+    for i, (src, dst) in enumerate(
+        [
+            (gw_hbm, gw), (feat_hbm, feat), (ld_hbm, ld_ref), (k_hbm, k_ref),
+            (q_hbm, q_ref), (v_hbm, v_ref), (ridge_hbm, ridge_ref),
+        ]
+    ):
+        c = pltpu.make_async_copy(src, dst, in_sem.at[i])
+        c.start()
+        loads.append(c)
+    loads[0].wait()
+    loads[1].wait()
     partial = nt(gw[...], feat[...])
     for j in range(nh):
         gsend[j] = partial[heads * j : heads * (j + 1)]
 
-    pl.semaphore_wait(barrier, nh - 1 + nz - 1 + ny - 1)
-
+    pl.semaphore_wait(barrier, nh - 1 + 2 + ny - 1)
+
+    signal(ready.at[0], at_z(1))
+    signal(ready.at[0], at_z(-1))
     gate_copies = []
     for d in range(1, nh):
         to = (me_h + d) % nh
-        c = pltpu.make_async_remote_copy(
-            src_ref=gsend.at[to], dst_ref=grecv.at[me_h], send_sem=gs_sem.at[d],
-            recv_sem=gr_sem.at[d], device_id={"head": to}, device_id_type=MESH,
+        gate_copies.append(
+            send(gsend.at[to], grecv.at[me_h], gs_sem.at[d], gr_sem.at[d], {"head": to})
         )
-        c.start()
-        gate_copies.append(c)
     grecv[me_h] = gsend[me_h]
 
+    loads[2].wait()
     within = jnp.concatenate([ld_ref[...]] * (8 // heads), axis=0)
     place = lax.broadcasted_iota(jnp.int32, (8, rows), 1) % BLOCK
     step = 1
     while step < BLOCK:
         within = within + jnp.where(place >= step, pltpu.roll(within, step, 1), 0.0)
         step *= 2
+    loads[3].wait()
     ksq = []
     for h in range(heads):
         kf = k_ref[:, h * width : (h + 1) * width].astype(F32)
@@ -100,13 +150,17 @@
     tail = jnp.exp(total_row - within)
     ltot = functools.reduce(lambda a, b: a + b, ends)
 
-    qunit, qinv = [], []
-    for h in range(heads):
-        qf = q_ref[:, h * width : (h + 1) * width].astype(F32)
-        root = jnp.sqrt(jnp.sum(qf * qf, axis=-1, keepdims=True) + 1e-06)
-        qunit.append(qf / root)
-        qinv.append(1.0 / root)
-
+    reach = 1
+    turn = 0
+    while 2 * reach <= nz // 2:
+        pl.semaphore_wait(ready.at[turn], 2)
+        reach *= 2
+        turn += 1
+        if 2 * reach <= nz // 2:
+            signal(ready.at[turn], at_z(reach))
+            signal(ready.at[turn], at_z(-reach))
+
+    loads[5].wait()
     for c in gate_copies:
         c.wait()
     logits = grecv[0]
@@ -127,7 +181,9 @@
     def values(h, b):
         return v_ref[b * BLOCK : (b + 1) * BLOCK, h * width : (h + 1) * width]
 
-    updates = []
+    order = sorted(range(1, nz), key=lambda d: -min(d, nz - d))
+    lane_row = lax.broadcasted_iota(jnp.int32, (1, width), 1)
+    updates, sends = [], []
     for h in range(heads):
         ups = []
         for b in range(blocks):
@@ -140,31 +196,39 @@
         total = ups[0]
         for b in range(1, blocks):
             total = total * jnp.exp(ends[b][h : h + 1]) + ups[b]
+        vkt, folded, diagonal = pack(total, width)
+        last = jnp.where(lane_row < width // 2, diagonal, ltot[h : h + 1])
         for c in range(nz):
-            sbuf[h, c, 0:part] = total[c * part : (c + 1) * part, 0:width]
-            sbuf[h, c, part : 2 * part] = total[c * part : (c + 1) * part, width:]
-            sbuf[h, c, 2 * part : 2 * part + 1] = jnp.broadcast_to(ltot[h : h + 1], (1, width))
-
-    msg = 2 * part + 1
-    sends = []
-    for h in range(heads):
+            sbuf[h, c, 0:part] = vkt[c * part : (c + 1) * part]
+            sbuf[h, c, part : part + fold] = folded[c * fold : (c + 1) * fold]
+            sbuf[h, c, part + fold : body_rows] = last
+        out = []
         for d in order:
             to = (me_z + d) % nz
-            c = pltpu.make_async_remote_copy(
-                src_ref=sbuf.at[h, to, pl.ds(0, msg)], dst_ref=rbuf.at[h, me_z, pl.ds(0, msg)],
-                send_sem=ss_sem.at[h, d], recv_sem=sr_sem.at[h, d],
-                device_id={"seq": me_y * nz + to}, device_id_type=MESH,
-            )
-            c.start()
-            sends.append(c)
+            out.append(
+                send(
+                    sbuf.at[h, to, pl.ds(0, body_rows)], rbuf.at[h, me_z, pl.ds(0, body_rows)],
+                    ss_sem.at[h, d], sr_sem.at[h, d], at_z(d),
+                )
+            )
+        sends.append(out)
         rbuf[h, me_z] = sbuf[h, me_z]
 
     lower = lax.broadcasted_iota(jnp.int32, (BLOCK, BLOCK), 0) >= lax.broadcasted_iota(
         jnp.int32, (BLOCK, BLOCK), 1
     )
+    loads[4].wait()
+    loads[6].wait()
+    qunit, qinv = [], []
+    for h in range(heads):
+        qf = q_ref[:, h * width : (h + 1) * width].astype(F32)
+        root = jnp.sqrt(jnp.sum(qf * qf, axis=-1, keepdims=True) + 1e-06)
+        qunit.append(qf / root)
+        qinv.append(1.0 / root)
     row1 = beta * kinv * kinv
     row2 = beta * kinv
-    for h in range(heads):
+
+    def prepare(h):
         for b in range(blocks):
             i = h * blocks + b
             sl = slice(b * BLOCK, (b + 1) * BLOCK)
@@ -179,64 +243,64 @@
             hi, lo = split(s * w1)
             in1_ref[i] = nn(hi, kb) + nn(lo, kb)
 
-    y_copies = []
-    for h in range(heads):
-        for d in range(1, nz):
-            sends[h * (nz - 1) + d - 1].wait()
-        state = jnp.zeros((2 * part, width), F32)
-        reach = jnp.zeros((1, width), F32)
+    def row_prefix(h):
+        for c in sends[h]:
+            c.wait()
+        state = jnp.zeros((body_rows, width), F32)
+        gone = jnp.zeros((1, 1), F32)
+        logs = []
         for z in range(nz):
-            tbuf[h, z, 0 : 2 * part] = state
-            tbuf[h, z, 2 * part : 2 * part + 1] = reach
-            log = rbuf[h, z, 2 * part : 2 * part + 1]
-            state = jnp.exp(log) * state + rbuf[h, z, 0 : 2 * part]
-            reach = reach + log
-        ybuf[h, 0 : 2 * part] = state
-        ybuf[h, 2 * part : 2 * part + 1] = reach
+            tbuf[h, z, 0:body_rows] = state
+            logs.append(gone)
+            chunk = rbuf[h, z, 0:body_rows]
+            log = chunk[part + fold : body_rows, width - 1 : width]
+            state = jnp.exp(log) * state + chunk
+            gone = gone + log
+        ybuf[h, 0:body_rows] = jnp.where(
+            (lax.broadcasted_iota(jnp.int32, (body_rows, width), 0) == body_rows - 1)
+            & (lax.broadcasted_iota(jnp.int32, (body_rows, width), 1) >= width // 2),
+            gone, state,
+        )
         yrecv[h, me_y] = ybuf[h]
-        for d in range(1, ny):
-            to = (me_y + d) % ny
-            c = pltpu.make_async_remote_copy(
-                src_ref=ybuf.at[h, pl.ds(0, msg)], dst_ref=yrecv.at[h, me_y, pl.ds(0, msg)],
-                send_sem=ys_sem.at[h, d], recv_sem=yr_sem.at[h, d],
-                device_id={"seq": to * nz + me_z}, device_id_type=MESH,
-            )
-            c.start()
-            y_copies.append(c)
-
-    returns = []
-    for h in range(heads):
-        for d in range(1, ny):
-            y_copies[h * (ny - 1) + d - 1].wait()
-        carry = jnp.zeros((2 * part, width), F32)
+        copies = [
+            send(
+                ybuf.at[h, pl.ds(0, body_rows)], yrecv.at[h, me_y, pl.ds(0, body_rows)],
+                ys_sem.at[h, d], yr_sem.at[h, d], at_y(d),
+            )
+            for d in range(1, ny)
+        ]
+        return logs, copies
+
+    def give_back(h, logs, copies):
+        for c in copies:
+            c.wait()
+        carry = jnp.zeros((body_rows, width), F32)
         for y in range(ny):
-            new = jnp.exp(yrecv[h, y, 2 * part : 2 * part + 1]) * carry + yrecv[h, y, 0 : 2 * part]
+            chunk = yrecv[h, y, 0:body_rows]
+            new = jnp.exp(chunk[part + fold : body_rows, width - 1 : width]) * carry + chunk
             carry = jnp.where(y < me_y, new, carry)
         for z in range(nz):
-            tbuf[h, z, 0 : 2 * part] = (
-                tbuf[h, z, 0 : 2 * part] + jnp.exp(tbuf[h, z, 2 * part : 2 * part + 1]) * carry
-            )
+            tbuf[h, z, 0:body_rows] = tbuf[h, z, 0:body_rows] + jnp.exp(logs[z]) * carry
+        out = []
         for d in order:
             to = (me_z + d) % nz
-            c = pltpu.make_async_remote_copy(
-                src_ref=tbuf.at[h, to, pl.ds(0, 2 * part)],
-                dst_ref=trecv.at[h, me_z, pl.ds(0, 2 * part)],
-                send_sem=ts_sem.at[h, d], recv_sem=tr_sem.at[h, d],
-                device_id={"seq": me_y * nz + to}, device_id_type=MESH,
-            )
-            c.start()
-            returns.append(c)
-        trecv[h, me_z] = tbuf[h, me_z, 0 : 2 * part]
-
-    for h in range(heads):
-        for d in range(1, nz):
-            returns[h * (nz - 1) + d - 1].wait()
-        start = jnp.concatenate(
-            [
-                trecv[h, :, 0:part].reshape(width, width),
-                trecv[h, :, part : 2 * part].reshape(width, width),
-            ],
-            axis=1,
+            out.append(
+                send(
+                    tbuf.at[h, to, pl.ds(0, body_rows)], trecv.at[h, me_z, pl.ds(0, body_rows)],
+                    ts_sem.at[h, d], tr_sem.at[h, d], at_z(d),
+                )
+            )
+        trecv[h, me_z] = tbuf[h, me_z]
+        return out
+
+    def solve(h, returns):
+        for c in returns:
+            c.wait()
+        start = unpack(
+            trecv[h, :, 0:part].reshape(width, width),
+            jnp.concatenate([trecv[h, c, part : part + fold] for c in range(nz)], axis=0),
+            trecv[h, 0, part + fold : body_rows],
+            width,
         )
         ridge = ridge_ref[h : h + 1]
         for b in range(blocks):
@@ -305,21 +369,33 @@
             )
             out_ref[sl, h * width : (h + 1) * width] = mixed.astype(BF16)
 
+    prepare(0)
+    logs0, copies0 = row_prefix(0)
+    pending = [give_back(0, logs0, copies0)]
+    for h in range(1, heads):
+        prepare(h)
+        logs, copies = row_prefix(h)
+        pending.append(give_back(h, logs, copies))
+    for h in range(heads):
+        solve(h, pending[h])
+
 
 def body(ny, nz, nh, features, gate_weight, queries, keys, values, log_decay, ridge):
-    rows = queries.shape[0]
+    rows, columns = queries.shape
     heads, width = ridge.shape
     blocks = rows // BLOCK
     part = width // nz
     vmem = pl.BlockSpec(memory_space=pltpu.VMEM)
-    pad = -(-(2 * part + 1) // 8) * 8
+    pad = -(-(part + part // 2 + 1) // 8) * 8
     dma = pltpu.SemaphoreType.DMA
+    ops = (features, gate_weight.T, queries, keys, values, log_decay.T, ridge)
     return pl.pallas_call(
         functools.partial(kernel, ny, nz, nh),
-        out_shape=jax.ShapeDtypeStruct((rows, heads * width), BF16),
-        in_specs=[vmem] * 7,
+        out_shape=jax.ShapeDtypeStruct((rows, columns), BF16),
+        in_specs=[pl.BlockSpec(memory_space=pl.ANY)] * 7,
         out_specs=vmem,
-        scratch_shapes=[
+        scratch_shapes=[pltpu.VMEM(o.shape, o.dtype) for o in ops]
+        + [
             pltpu.VMEM((nh, heads, rows), F32),
             pltpu.VMEM((nh, heads, rows), F32),
             pltpu.VMEM((heads, nz, pad, width), F32),
@@ -327,17 +403,18 @@
             pltpu.VMEM((heads, pad, width), F32),
             pltpu.VMEM((heads, ny, pad, width), F32),
             pltpu.VMEM((heads, nz, pad, width), F32),
-            pltpu.VMEM((heads, nz, 2 * part, width), F32),
+            pltpu.VMEM((heads, nz, pad, width), F32),
             pltpu.VMEM((heads * blocks, BLOCK, BLOCK), F32),
             pltpu.VMEM((heads * blocks, BLOCK, BLOCK), F32),
             pltpu.VMEM((heads * blocks, BLOCK, BLOCK), F32),
             pltpu.VMEM((heads * blocks, BLOCK, width), F32),
+            dma((7,)), pltpu.SemaphoreType.REGULAR((4,)),
             dma((nh,)), dma((nh,)), dma((heads, nz)), dma((heads, nz)),
             dma((heads, ny)), dma((heads, ny)), dma((heads, nz)), dma((heads, nz)),
         ],
         compiler_params=pltpu.CompilerParams(collective_id=0, has_side_effects=True),
         name="mesa",
-    )(features, gate_weight.T, queries, keys, values, log_decay.T, ridge)
+    )(*ops)
 
 
 def solution(mesh):

time: 57.1 us -> 51.3 us (0.90); the launches traced: 56.8 us -> 50.4 us
  Pallas kernels: 55.1 us -> 48.7 us
    pallas_call x1, Pallas kernels: 55.1 us -> 48.7 us  [body(): pl.pallas_call(functools.partial(kernel, ny, nz, nh), out_shape=jax.Shape...]
where the time goes in v2:
time: 51.3 us; the launch traced here: 50.4 us
  Pallas kernels  48.7 us (95%)
  local copies, waits for them, and re-layouts  1.67 us (3%)
    pallas_call x1, Pallas kernels, body(): pl.pallas_call(functools.partial(kernel, ny, nz, nh), out_shape=jax.Shape...  48.7 us
    unnamed x1, local copies, waits for them, and re-layouts  1.67 us

profile of v2, /device:TPU:24, one launch (start us, length us, event | category | flops | bytes accessed | tf_op | source)
XLA Modules:
  0.0 50.4 jit_solution(16802323317609112553)
XLA Ops:
  0.0 48.7 %mesa.1 = bf16[512,256]{1,0:T(8,128)(2,1)} custom-call(bf16[512,256]{1,0:T(8,128)(2,1)} %feat_hbm.1, bf16[16,256]{1,0:T(8,128)(2,1)} %bitcast.2, bf16[512,256]{1,0:T(8,128)(2,1)} %q_hbm.1, bf16[512,256]{1,0:T(8,128)(2,1)} %k_hbm.1, bf16[512,256]{1,0:T(8,128)(2,1)} %v_hbm.1, f32[2,512]{1,0:T(2,128)} %bitcast.3, f32[2,128]{1,0:T(2,128)} %ridge_hbm.1), custom_call_target="tpu_custom_call" | custom-call | tf_op jit(solution)/shard_map/mesa/pallas_call | solution.py:392
  48.7 1.7 %copy.9 = bf16[512,256]{1,0:T(8,128)(2,1)} copy(bf16[512,256]{1,0:T(8,128)(2,1)} %mesa.1) | data formatting | bytes 524288

commit v3 on v2

v3 whole, which is shorter than its diff:
```python
import functools

import jax
import jax.numpy as jnp
from jax import lax
from jax.experimental import pallas as pl
from jax.experimental.pallas import tpu as pltpu
from jax.sharding import PartitionSpec as P

CG_STEPS = 4
BLOCK = 256
MESH = pl.DeviceIdType.MESH
F32 = jnp.float32
BF16 = jnp.bfloat16


def nn(a, b):
    return jnp.dot(a, b, preferred_element_type=F32)


def nt(a, b):
    return lax.dot_general(a, b, (((1,), (1,)), ((), ())), preferred_element_type=F32)


def tn(a, b):
    return lax.dot_general(a, b, (((0,), (0,)), ((), ())), preferred_element_type=F32)


def split(a):
    hi = a.astype(BF16)
    return hi, (a - hi.astype(F32)).astype(BF16)


def column_sums(sq):
    ones = jnp.ones((8, sq.shape[1]), BF16)
    hi, lo = split(sq)
    return nt(ones, hi) + nt(ones, lo)


def pack(total, width):
    half = width // 2
    lane = lax.broadcasted_iota(jnp.int32, (half, width), 1)
    row = lax.broadcasted_iota(jnp.int32, (half, width), 0)
    top = total[0:half]
    turned = pltpu.roll(total[half:width], half, 1)
    folded = jnp.where(lane >= row, top, turned)
    diagonal = jnp.sum(jnp.where(lane == row, turned, 0.0), axis=0, keepdims=True)
    return folded, diagonal


def unpack(folded, diagonal, width):
    half = width // 2
    lane = lax.broadcasted_iota(jnp.int32, (half, width), 1)
    row = lax.broadcasted_iota(jnp.int32, (half, width), 0)
    flipped = jnp.transpose(jnp.concatenate([folded, jnp.zeros_like(folded)], axis=0))
    top = jnp.where(lane >= row, folded, flipped[0:half])
    corner = jnp.where(lane == row, diagonal, jnp.where(lane < row, folded, flipped[0:half]))
    bottom = jnp.where(lane < half, flipped[half:width], pltpu.roll(corner, half, 1))
    return jnp.concatenate([top, bottom], axis=0)


def kernel(
    ny, nz, nh, feat_hbm, gw_hbm, q_hbm, k_hbm, v_hbm, ld_hbm, ridge_hbm, out_ref,
    feat, gw, q_ref, k_ref, v_ref, ld_ref, ridge_ref,
    gsend, grecv, sbuf, rbuf, ybuf, yrecv, carry_ref, tbuf, trecv, kt_ref, w1_ref, w2_ref, s1_ref, in1_ref,
    in_sem, ready, gs_sem, gr_sem, ss_sem, sr_sem, ys_sem, yr_sem, ts_sem, tr_sem,
):
    rows = q_ref.shape[0]
    heads = ridge_ref.shape[0]
    width = ridge_ref.shape[1]
    blocks = rows // BLOCK
    part = width // nz
    fold = part // 2
    counts = (heads * (fold + 1), heads * part)
    seq = lax.axis_index("seq")
    me_h = lax.axis_index("head")
    me_y = seq // nz
    me_z = seq % nz

    def at_z(d):
        return {"seq": me_y * nz + (me_z + d + nz) % nz}

    def at_y(d):
        return {"seq": ((me_y + d) % ny) * nz + me_z}

    def signal(sem, where):
        pl.semaphore_signal(sem, inc=1, device_id=where, device_id_type=MESH)

    def send(src, dst, sem_out, sem_in, where):
        c = pltpu.make_async_remote_copy(
            src_ref=src, dst_ref=dst, send_sem=sem_out, recv_sem=sem_in,
            device_id=where, device_id_type=MESH,
        )
        c.start()
        return c

    barrier = pltpu.get_barrier_semaphore()
    for d in range(1, nh):
        signal(barrier, {"head": (me_h + d) % nh})
    near = sorted({d % nz for d in (1, -1, 2, -2)} - {0})
    for d in near:
        signal(barrier, at_z(d))
    for d in range(1, ny):
        signal(barrier, at_y(d))

    loads = []
    for i, (src, dst) in enumerate(
        [
            (gw_hbm, gw), (feat_hbm, feat), (ld_hbm, ld_ref), (k_hbm, k_ref),
            (q_hbm, q_ref), (v_hbm, v_ref), (ridge_hbm, ridge_ref),
        ]
    ):
        c = pltpu.make_async_copy(src, dst, in_sem.at[i])
        c.start()
        loads.append(c)
    loads[0].wait()
    loads[1].wait()
    partial = nt(gw[...], feat[...])
    for j in range(nh):
        gsend[j] = partial[heads * j : heads * (j + 1)]

    pl.semaphore_wait(barrier, nh - 1 + len(near) + ny - 1)

    spans = [r for r in (2, 4, 8, 16) if r < nz // 2]
    if spans:
        signal(ready.at[0], at_z(spans[0]))
        signal(ready.at[0], at_z(-spans[0]))
    gate_copies = []
    for d in range(1, nh):
        to = (me_h + d) % nh
        gate_copies.append(
            send(gsend.at[to], grecv.at[me_h], gs_sem.at[d], gr_sem.at[d], {"head": to})
        )
    grecv[me_h] = gsend[me_h]

    loads[2].wait()
    within = jnp.concatenate([ld_ref[...]] * (8 // heads), axis=0)
    place = lax.broadcasted_iota(jnp.int32, (8, rows), 1) % BLOCK
    step = 1
    while step < BLOCK:
        within = within + jnp.where(place >= step, pltpu.roll(within, step, 1), 0.0)
        step *= 2
    loads[3].wait()
    ksq = []
    for h in range(heads):
        kf = k_ref[:, h * width : (h + 1) * width].astype(F32)
        ksq.append(column_sums(kf * kf)[0:1])
    knorm = jnp.sqrt(jnp.concatenate(ksq, axis=0) + 1e-06)
    kinv = 1.0 / knorm
    within = within[0:heads]
    ends = [within[:, (b + 1) * BLOCK - 1 : (b + 1) * BLOCK] for b in range(blocks)]
    total_row = jnp.concatenate([jnp.broadcast_to(e, (heads, BLOCK)) for e in ends], axis=1)
    tail = jnp.exp(total_row - within)
    ltot = functools.reduce(lambda a, b: a + b, ends)
    both_rows = jnp.concatenate([within, jnp.exp(within)], axis=0)
    cols = jnp.transpose(jnp.concatenate([both_rows] * (128 // (2 * heads)), axis=0))

    def col(kind, h, b):
        return cols[b * BLOCK : (b + 1) * BLOCK, kind * heads + h : kind * heads + h + 1]

    for h in range(heads):
        kt_ref[h] = jnp.transpose(k_ref[:, h * width : (h + 1) * width].astype(F32))

    for turn in range(1, len(spans)):
        pl.semaphore_wait(ready.at[turn - 1], 2)
        signal(ready.at[turn], at_z(spans[turn]))
        signal(ready.at[turn], at_z(-spans[turn]))

    loads[5].wait()
    for c in gate_copies:
        c.wait()
    logits = grecv[0]
    for j in range(1, nh):
        logits = logits + grecv[j]
    beta = 1.0 / (1.0 + jnp.exp(-logits))
    vfac = tail * beta * kinv
    kfac = vfac * kinv

    def keys(h, b):
        return k_ref[b * BLOCK : (b + 1) * BLOCK, h * width : (h + 1) * width]

    def values(h, b):
        return v_ref[b * BLOCK : (b + 1) * BLOCK, h * width : (h + 1) * width]

    order = sorted(range(1, nz), key=lambda d: -min(d, nz - d))
    lane_row = lax.broadcasted_iota(jnp.int32, (1, width), 1)
    sends = []

    def state_update(h, factor, right):
        ups = []
        for b in range(blocks):
            sl = slice(b * BLOCK, (b + 1) * BLOCK)
            hi, lo = split(kt_ref[h, :, sl] * factor[h : h + 1, sl])
            prod = nn(jnp.concatenate([hi, lo], axis=0), right(h, b))
            ups.append(prod[:width] + prod[width:])
        total = ups[0]
        for b in range(1, blocks):
            total = total * jnp.exp(ends[b][h : h + 1]) + ups[b]
        return ups, total

    def hand_in(piece):
        out = []
        for d in order:
            to = (me_z + d) % nz
            out.append(
                send(
                    sbuf.at[piece, to, pl.ds(0, counts[piece])],
                    rbuf.at[piece, me_z, pl.ds(0, counts[piece])],
                    ss_sem.at[piece, d], sr_sem.at[piece, d], at_z(d),
                )
            )
        sends.append(out)
        rbuf[piece, me_z] = sbuf[piece, me_z]

    kk_ups, vk_ups = [], []
    for h in range(heads):
        ups, total = state_update(h, kfac, keys)
        kk_ups.append(ups)
        folded, diagonal = pack(total, width)
        last = jnp.where(lane_row < width // 2, diagonal, ltot[h : h + 1])
        for c in range(nz):
            sbuf[0, c, h * fold : (h + 1) * fold] = folded[c * fold : (c + 1) * fold]
            sbuf[0, c, heads * fold + h : heads * fold + h + 1] = last
    if spans:
        pl.semaphore_wait(ready.at[len(spans) - 1], 2)
    hand_in(0)
    for h in range(heads):
        ups, total = state_update(h, vfac, values)
        vk_ups.append(ups)
        for c in range(nz):
            sbuf[1, c, h * part : (h + 1) * part] = total[c * part : (c + 1) * part]
    hand_in(1)

    lower = lax.broadcasted_iota(jnp.int32, (BLOCK, BLOCK), 0) >= lax.broadcasted_iota(
        jnp.int32, (BLOCK, BLOCK), 1
    )
    loads[4].wait()
    loads[6].wait()
    qunit, qinv = [], []
    for h in range(heads):
        qf = q_ref[:, h * width : (h + 1) * width].astype(F32)
        root = jnp.sqrt(jnp.sum(qf * qf, axis=-1, keepdims=True) + 1e-06)
        qunit.append(qf / root)
        qinv.append(1.0 / root)
    row1 = beta * kinv * kinv
    row2 = beta * kinv

    def prepare(h):
        for b in range(blocks):
            i = h * blocks + b
            sl = slice(b * BLOCK, (b + 1) * BLOCK)
            spread = col(0, h, b) - within[h : h + 1, sl]
            decay = jnp.where(lower, jnp.exp(jnp.minimum(spread, 0.0)), 0.0)
            w1 = decay * row1[h : h + 1, sl]
            w1_ref[i] = w1
            w2_ref[i] = decay * row2[h : h + 1, sl]
            kb = keys(h, b)
            s = nt(q_ref[sl, h * width : (h + 1) * width], kb) * qinv[h][sl]
            s1_ref[i] = s
            hi, lo = split(s * w1)
            in1_ref[i] = nn(hi, kb) + nn(lo, kb)

    def row_gain(piece, logs):
        row = lax.broadcasted_iota(jnp.int32, (counts[piece], 1), 0)
        own = row >= part if piece else ((row >= fold) & (row < heads * fold)) | (row > heads * fold)
        return jnp.exp(jnp.where(own, logs[1], logs[0]))

    def logs_of(chunk):
        return [chunk[heads * fold + h : heads * fold + h + 1, width - 1 : width] for h in range(heads)]

    def y_copy(piece, source, target):
        return pltpu.make_async_remote_copy(
            src_ref=ybuf.at[piece, pl.ds(0, counts[piece])],
            dst_ref=yrecv.at[piece, source, pl.ds(0, counts[piece])],
            send_sem=ys_sem.at[piece, target], recv_sem=yr_sem.at[piece, source],
            device_id={"seq": target * nz + me_z}, device_id_type=MESH,
        )

    def row_prefix(piece):
        for c in sends[piece]:
            c.wait()
        n = counts[piece]
        state = jnp.zeros((n, width), F32)
        gone = [jnp.zeros((1, 1), F32)] * heads
        before = []
        for z in range(nz):
            tbuf[piece, z, 0:n] = state
            before.append(gone)
            logs = logs_of(rbuf[0, z, 0 : counts[0]])
            state = row_gain(piece, logs) * state + rbuf[piece, z, 0:n]
            gone = [g + w for g, w in zip(gone, logs)]
        ybuf[piece, 0:n] = state
        if piece == 0:
            for h in range(heads):
                r = heads * fold + h
                ybuf[0, r : r + 1] = jnp.where(lane_row < width // 2, state[r : r + 1], gone[h])
        for y in range(1, ny):

            @pl.when(me_y < y)
            def _():
                y_copy(piece, me_y, y).start()

        return before

    def give_back(piece, before):
        n = counts[piece]
        carry_ref[piece] = jnp.zeros(carry_ref.shape[1:], F32)
        for y in range(ny - 1):

            @pl.when(y < me_y)
            def _():
                y_copy(piece, y, me_y).wait_recv()
                gain = row_gain(piece, logs_of(yrecv[0, y, 0 : counts[0]]))
                carry_ref[piece, 0:n] = gain * carry_ref[piece, 0:n] + yrecv[piece, y, 0:n]

        carry = carry_ref[piece, 0:n]
        for z in range(nz):
            tbuf[piece, z, 0:n] = tbuf[piece, z, 0:n] + row_gain(piece, before[z]) * carry
        trecv[piece, me_z] = tbuf[piece, me_z]

    def t_copy(piece, to):
        d = (to - me_z + nz) % nz
        return pltpu.make_async_remote_copy(
            src_ref=tbuf.at[piece, to, pl.ds(0, counts[piece])],
            dst_ref=trecv.at[piece, me_z, pl.ds(0, counts[piece])],
            send_sem=ts_sem.at[piece, d], recv_sem=tr_sem.at[piece, d],
            device_id={"seq": me_y * nz + to}, device_id_type=MESH,
        )

    def hand_out(piece, first, last):
        for to in range(first, last):

            @pl.when(to != me_z)
            def _():
                t_copy(piece, to).start()

    bands = [slice(m, m + BLOCK // 2) for m in range(0, BLOCK, BLOCK // 2)]

    def local(scores, weights, i, tall):
        return jnp.concatenate(
            [
                nn(jnp.concatenate(split(u * weights[i, band, 0 : band.stop]), axis=1), t)
                for u, band, t in zip(scores, bands, tall)
            ],
            axis=0,
        )

    def starts(incoming, ups, h):
        out = [incoming]
        for b in range(1, blocks):
            out.append(out[-1] * jnp.exp(ends[b - 1][h : h + 1]) + ups[h][b - 1])
        return out

    def tall(a):
        hi, lo = split(a)
        return jnp.concatenate([hi, hi, lo], axis=0)

    def wide(a):
        hi, lo = split(a)
        return jnp.concatenate([hi, lo, hi], axis=1)

    def solve(hs):
        runs = []
        for h in hs:
            incoming = unpack(
                jnp.concatenate(
                    [trecv[0, c, h * fold : (h + 1) * fold] for c in range(nz)], axis=0
                ),
                trecv[0, 0, heads * fold + h : heads * fold + h + 1],
                width,
            )
            for b, start in enumerate(starts(incoming, kk_ups, h)):
                sl = slice(b * BLOCK, (b + 1) * BLOCK)
                kb = keys(h, b)
                q = qunit[h][sl]
                runs.append(
                    dict(
                        h=h, b=b, i=h * blocks + b, sl=sl, kk=tall(start), lead=col(1, h, b),
                        k_wide=jnp.concatenate([kb, kb], axis=1), p=q, r=q,
                        k_tall=[jnp.concatenate([kb[: m.stop]] * 2, axis=0) for m in bands],
                        norm=jnp.sum(q * q, axis=-1, keepdims=True), ridge=ridge_ref[h : h + 1],
                    )
                )
        for step in range(CG_STEPS):
            for c in runs:
                if step == 0:
                    h = c["h"]
                    q = q_ref[c["sl"], h * width : (h + 1) * width]
                    got = nn(jnp.concatenate([q, q], axis=1), c["kk"][width:])
                    c["state"] = got * (c["lead"] * qinv[h][c["sl"]])
                    c["s"] = [s1_ref[c["i"], top, 0 : top.stop] for top in bands]
                else:
                    three = wide(c["p"])
                    pair = three[:, : 2 * width]
                    c["s"] = [nt(pair[band], c["k_wide"][: band.stop]) for band in bands]
                    c["state"] = c["lead"] * nn(three, c["kk"])
            for c in runs:
                c["near"] = c["state"] + c["ridge"] * c["p"]
                if step == 0:
                    c["image"] = c["near"] + in1_ref[c["i"]]
                elif step < CG_STEPS - 1:
                    c["image"] = c["near"] + local(c["s"], w1_ref, c["i"], c["k_tall"])
            for c in runs:
                p, s = c["p"], c["s"]
                if step == CG_STEPS - 1:
                    energy = jnp.sum(p * c["near"], axis=-1, keepdims=True) + jnp.concatenate(
                        [
                            jnp.sum(u * (u * w1_ref[c["i"], band, 0 : band.stop]), axis=-1, keepdims=True)
                            for u, band in zip(s, bands)
                        ],
                        axis=0,
                    )
                else:
                    energy = jnp.sum(p * c["image"], axis=-1, keepdims=True)
                alpha = c["norm"] / energy
                c["x"] = alpha * p if step == 0 else c["x"] + alpha * p
                scaled = [alpha[band] * u for u, band in zip(s, bands)]
                c["sum"] = scaled if step == 0 else [u + w for u, w in zip(c["sum"], scaled)]
                if step < CG_STEPS - 1:
                    c["r"] = c["r"] - alpha * c["image"]
                    after = jnp.sum(c["r"] * c["r"], axis=-1, keepdims=True)
                    c["p"] = c["r"] + (after / c["norm"]) * p
                    c["norm"] = after
        return runs

    def read_out(runs):
        for h in range(heads):
            incoming = trecv[1, :, h * part : (h + 1) * part].reshape(width, width)
            for c, start in zip(runs[h * blocks : (h + 1) * blocks], starts(incoming, vk_ups, h)):
                vb = values(h, c["b"])
                v_tall = [jnp.concatenate([vb[: m.stop]] * 2, axis=0) for m in bands]
                mixed = c["lead"] * nn(wide(c["x"]), tall(start)) + local(
                    c["sum"], w2_ref, c["i"], v_tall
                )
                out_ref[c["sl"], h * width : (h + 1) * width] = mixed.astype(BF16)

    def arrived(piece):
        for d in range(1, nz):
            t_copy(piece, (me_z + d) % nz).wait_recv()

    early = nz // 2
    for h in range(heads):
        prepare(h)
    for piece in range(2):
        give_back(piece, row_prefix(piece))
        hand_out(piece, 0, early)
    for piece in range(2):
        hand_out(piece, early, nz)
    arrived(0)
    runs = solve(range(heads))
    arrived(1)
    read_out(runs)
    for piece in range(2):
        for d in range(1, nz):
            t_copy(piece, (me_z + d) % nz).wait_send()
        for y in range(1, ny):

            @pl.when(me_y < y)
            def _():
                y_copy(piece, me_y, y).wait_send()


def body(ny, nz, nh, features, gate_weight, queries, keys, values, log_decay, ridge):
    rows, columns = queries.shape
    heads, width = ridge.shape
    blocks = rows // BLOCK
    part = width // nz
    vmem = pl.BlockSpec(memory_space=pltpu.VMEM)
    pad = -(-(heads * part) // 8) * 8
    dma = pltpu.SemaphoreType.DMA
    ops = (features, gate_weight.T, queries, keys, values, log_decay.T, ridge)
    return pl.pallas_call(
        functools.partial(kernel, ny, nz, nh),
        out_shape=jax.ShapeDtypeStruct((rows, columns), BF16),
        in_specs=[pl.BlockSpec(memory_space=pl.ANY)] * 7,
        out_specs=vmem,
        scratch_shapes=[pltpu.VMEM(o.shape, o.dtype) for o in ops]
        + [
            pltpu.VMEM((nh, heads, rows), F32),
            pltpu.VMEM((nh, heads, rows), F32),
            pltpu.VMEM((2, nz, pad, width), F32),
            pltpu.VMEM((2, nz, pad, width), F32),
            pltpu.VMEM((2, pad, width), F32),
            pltpu.VMEM((2, ny, pad, width), F32),
            pltpu.VMEM((2, pad, width), F32),
            pltpu.VMEM((2, nz, pad, width), F32),
            pltpu.VMEM((2, nz, pad, width), F32),
            pltpu.VMEM((heads, width, rows), F32),
            pltpu.VMEM((heads * blocks, BLOCK, BLOCK), F32),
            pltpu.VMEM((heads * blocks, BLOCK, BLOCK), F32),
            pltpu.VMEM((heads * blocks, BLOCK, BLOCK), F32),
            pltpu.VMEM((heads * blocks, BLOCK, width), F32),
            dma((7,)), pltpu.SemaphoreType.REGULAR((4,)),
            dma((nh,)), dma((nh,)), dma((2, nz)), dma((2, nz)),
            dma((2, ny)), dma((2, ny)), dma((2, nz)), dma((2, nz)),
        ],
        compiler_params=pltpu.CompilerParams(collective_id=0, has_side_effects=True),
        name="mesa",
    )(*ops)


def solution(mesh):
    seq, nh = mesh.shape["seq"], mesh.shape["head"]
    nz = 16 if seq >= 64 else seq // 2
    placed = (
        P("seq", "head"),
        P("head", None),
        P("seq", "head"),
        P("seq", "head"),
        P("seq", "head"),
        P("seq", "head"),
        P("head", None),
    )
    return jax.shard_map(
        functools.partial(body, seq // nz, nz, nh),
        mesh=mesh, in_specs=placed, out_specs=P("seq", "head"), check_vma=False,
    )
```

time: 51.3 us -> 46.9 us (0.914); the launches traced: 50.4 us -> 46.7 us
  Pallas kernels: 48.7 us -> 45 us
    pallas_call x1, Pallas kernels: 48.7 us -> 45 us  [body(): pl.pallas_call(functools.partial(kernel, ny, nz, nh), out_shape=jax.Shape...]
where the time goes in v3:
time: 46.9 us; the launch traced here: 46.7 us
  Pallas kernels  45 us (96%)
  local copies, waits for them, and re-layouts  1.67 us (4%)
    pallas_call x1, Pallas kernels, body(): pl.pallas_call(functools.partial(kernel, ny, nz, nh), out_shape=jax.Shape...  45 us
    unnamed x1, local copies, waits for them, and re-layouts  1.67 us

profile of v3, /device:TPU:24, one launch (start us, length us, event | category | flops | bytes accessed | tf_op | source)
XLA Modules:
  0.0 46.7 jit_solution(10062664266665155804)
XLA Ops:
  0.0 45.0 %mesa.1 = bf16[512,256]{1,0:T(8,128)(2,1)} custom-call(bf16[512,256]{1,0:T(8,128)(2,1)} %feat_hbm.1, bf16[16,256]{1,0:T(8,128)(2,1)} %bitcast.2, bf16[512,256]{1,0:T(8,128)(2,1)} %q_hbm.1, bf16[512,256]{1,0:T(8,128)(2,1)} %k_hbm.1, bf16[512,256]{1,0:T(8,128)(2,1)} %v_hbm.1, f32[2,512]{1,0:T(2,128)} %bitcast.3, f32[2,128]{1,0:T(2,128)} %ridge_hbm.1), custom_call_target="tpu_custom_call" | custom-call | tf_op jit(solution)/shard_map/mesa/pallas_call | solution.py:472
  45.0 1.7 %copy.9 = bf16[512,256]{1,0:T(8,128)(2,1)} copy(bf16[512,256]{1,0:T(8,128)(2,1)} %mesa.1) | data formatting | bytes 524288

commit v4 on v3

--- a/solution.py
+++ b/solution.py
@@ -71,7 +71,10 @@
     blocks = rows // BLOCK
     part = width // nz
     fold = part // 2
-    counts = (heads * (fold + 1), heads * part)
+    extra = heads * fold
+    counts = (extra + 1, heads * part)
+    half = width // 2
+    log_lane = (half, half + half // heads)
     seq = lax.axis_index("seq")
     me_h = lax.axis_index("head")
     me_y = seq // nz
@@ -110,11 +113,13 @@
             (q_hbm, q_ref), (v_hbm, v_ref), (ridge_hbm, ridge_ref),
         ]
     ):
-        c = pltpu.make_async_copy(src, dst, in_sem.at[i])
+        loads.append(pltpu.make_async_copy(src, dst, in_sem.at[i]))
+    for c in loads[:3]:
         c.start()
-        loads.append(c)
     loads[0].wait()
     loads[1].wait()
+    for c in loads[3:]:
+        c.start()
     partial = nt(gw[...], feat[...])
     for j in range(nh):
         gsend[j] = partial[heads * j : heads * (j + 1)]
@@ -184,8 +189,6 @@
 
     order = sorted(range(1, nz), key=lambda d: -min(d, nz - d))
     lane_row = lax.broadcasted_iota(jnp.int32, (1, width), 1)
-    sends = []
-
     def state_update(h, factor, right):
         ups = []
         for b in range(blocks):
@@ -198,38 +201,49 @@
             total = total * jnp.exp(ends[b][h : h + 1]) + ups[b]
         return ups, total
 
+    def s_copy(piece, d):
+        return pltpu.make_async_remote_copy(
+            src_ref=sbuf.at[piece, (me_z + d) % nz, pl.ds(0, counts[piece])],
+            dst_ref=rbuf.at[piece, me_z, pl.ds(0, counts[piece])],
+            send_sem=ss_sem.at[piece, d], recv_sem=sr_sem.at[piece, d],
+            device_id=at_z(d), device_id_type=MESH,
+        )
+
     def hand_in(piece):
-        out = []
         for d in order:
-            to = (me_z + d) % nz
-            out.append(
-                send(
-                    sbuf.at[piece, to, pl.ds(0, counts[piece])],
-                    rbuf.at[piece, me_z, pl.ds(0, counts[piece])],
-                    ss_sem.at[piece, d], sr_sem.at[piece, d], at_z(d),
-                )
-            )
-        sends.append(out)
-        rbuf[piece, me_z] = sbuf[piece, me_z]
-
-    kk_ups, vk_ups = [], []
+            s_copy(piece, d).start()
+
+    def handed_in(piece):
+        for d in order:
+            s_copy(piece, d).wait_recv()
+
+    kk_ups, vk_ups, diagonals = [], [], []
     for h in range(heads):
         ups, total = state_update(h, kfac, keys)
         kk_ups.append(ups)
         folded, diagonal = pack(total, width)
-        last = jnp.where(lane_row < width // 2, diagonal, ltot[h : h + 1])
+        diagonals.append(diagonal)
         for c in range(nz):
             sbuf[0, c, h * fold : (h + 1) * fold] = folded[c * fold : (c + 1) * fold]
-            sbuf[0, c, heads * fold + h : heads * fold + h + 1] = last
+    logs_row = jnp.where(lane_row < log_lane[1], ltot[0:1], ltot[1:2])
+    for c in range(nz):
+        sbuf[0, c, extra : extra + 1] = jnp.where(lane_row < half, diagonals[min(c, 1)], logs_row)
     if spans:
         pl.semaphore_wait(ready.at[len(spans) - 1], 2)
     hand_in(0)
+    rbuf[0, me_z] = sbuf[0, me_z]
     for h in range(heads):
         ups, total = state_update(h, vfac, values)
         vk_ups.append(ups)
         for c in range(nz):
             sbuf[1, c, h * part : (h + 1) * part] = total[c * part : (c + 1) * part]
-    hand_in(1)
+    rbuf[1, me_z] = sbuf[1, me_z]
+
+    at_once = me_h % 2 == 0
+
+    @pl.when(at_once)
+    def _():
+        hand_in(1)
 
     lower = lax.broadcasted_iota(jnp.int32, (BLOCK, BLOCK), 0) >= lax.broadcasted_iota(
         jnp.int32, (BLOCK, BLOCK), 1
@@ -262,11 +276,14 @@
 
     def row_gain(piece, logs):
         row = lax.broadcasted_iota(jnp.int32, (counts[piece], 1), 0)
-        own = row >= part if piece else ((row >= fold) & (row < heads * fold)) | (row > heads * fold)
-        return jnp.exp(jnp.where(own, logs[1], logs[0]))
+        if piece:
+            second = row >= part
+        else:
+            second = (row >= fold) & (row < extra) | (row == extra) & (me_z > 0)
+        return jnp.exp(jnp.where(second, logs[1], logs[0]))
 
     def logs_of(chunk):
-        return [chunk[heads * fold + h : heads * fold + h + 1, width - 1 : width] for h in range(heads)]
+        return [chunk[extra : extra + 1, at : at + 1] for at in log_lane]
 
     def y_copy(piece, source, target):
         return pltpu.make_async_remote_copy(
@@ -277,8 +294,8 @@
         )
 
     def row_prefix(piece):
-        for c in sends[piece]:
-            c.wait()
+        if piece == 1:
+            handed_in(1)
         n = counts[piece]
         state = jnp.zeros((n, width), F32)
         gone = [jnp.zeros((1, 1), F32)] * heads
@@ -291,9 +308,8 @@
             gone = [g + w for g, w in zip(gone, logs)]
         ybuf[piece, 0:n] = state
         if piece == 0:
-            for h in range(heads):
-                r = heads * fold + h
-                ybuf[0, r : r + 1] = jnp.where(lane_row < width // 2, state[r : r + 1], gone[h])
+            ends_row = jnp.where(lane_row < log_lane[1], gone[0], gone[1])
+            ybuf[0, extra : extra + 1] = jnp.where(lane_row < half, state[extra : extra + 1], ends_row)
         for y in range(1, ny):
 
             @pl.when(me_y < y)
@@ -302,7 +318,7 @@
 
         return before
 
-    def give_back(piece, before):
+    def give_back(piece):
         n = counts[piece]
         carry_ref[piece] = jnp.zeros(carry_ref.shape[1:], F32)
         for y in range(ny - 1):
@@ -313,10 +329,15 @@
                 gain = row_gain(piece, logs_of(yrecv[0, y, 0 : counts[0]]))
                 carry_ref[piece, 0:n] = gain * carry_ref[piece, 0:n] + yrecv[piece, y, 0:n]
 
+    def hand_out(piece, before, first, last):
+        n = counts[piece]
         carry = carry_ref[piece, 0:n]
-        for z in range(nz):
+        for z in range(first, last):
             tbuf[piece, z, 0:n] = tbuf[piece, z, 0:n] + row_gain(piece, before[z]) * carry
-        trecv[piece, me_z] = tbuf[piece, me_z]
+
+            @pl.when(z != me_z)
+            def _():
+                t_copy(piece, z).start()
 
     def t_copy(piece, to):
         d = (to - me_z + nz) % nz
@@ -327,13 +348,6 @@
             device_id={"seq": me_y * nz + to}, device_id_type=MESH,
         )
 
-    def hand_out(piece, first, last):
-        for to in range(first, last):
-
-            @pl.when(to != me_z)
-            def _():
-                t_copy(piece, to).start()
-
     bands = [slice(m, m + BLOCK // 2) for m in range(0, BLOCK, BLOCK // 2)]
 
     def local(scores, weights, i, tall):
@@ -366,7 +380,7 @@
                 jnp.concatenate(
                     [trecv[0, c, h * fold : (h + 1) * fold] for c in range(nz)], axis=0
                 ),
-                trecv[0, 0, heads * fold + h : heads * fold + h + 1],
+                trecv[0, h, extra : extra + 1],
                 width,
             )
             for b, start in enumerate(starts(incoming, kk_ups, h)):
@@ -414,24 +428,25 @@
                     energy = jnp.sum(p * c["image"], axis=-1, keepdims=True)
                 alpha = c["norm"] / energy
                 c["x"] = alpha * p if step == 0 else c["x"] + alpha * p
-                scaled = [alpha[band] * u for u, band in zip(s, bands)]
-                c["sum"] = scaled if step == 0 else [u + w for u, w in zip(c["sum"], scaled)]
                 if step < CG_STEPS - 1:
                     c["r"] = c["r"] - alpha * c["image"]
                     after = jnp.sum(c["r"] * c["r"], axis=-1, keepdims=True)
                     c["p"] = c["r"] + (after / c["norm"]) * p
                     c["norm"] = after
+        for c in runs:
+            c["x_wide"] = wide(c["x"])
+            pair = c["x_wide"][:, : 2 * width]
+            x_scores = [nt(pair[band], c["k_wide"][: band.stop]) for band in bands]
+            vb = values(c["h"], c["b"])
+            v_tall = [jnp.concatenate([vb[: m.stop]] * 2, axis=0) for m in bands]
+            c["near"] = local(x_scores, w2_ref, c["i"], v_tall)
         return runs
 
     def read_out(runs):
         for h in range(heads):
             incoming = trecv[1, :, h * part : (h + 1) * part].reshape(width, width)
             for c, start in zip(runs[h * blocks : (h + 1) * blocks], starts(incoming, vk_ups, h)):
-                vb = values(h, c["b"])
-                v_tall = [jnp.concatenate([vb[: m.stop]] * 2, axis=0) for m in bands]
-                mixed = c["lead"] * nn(wide(c["x"]), tall(start)) + local(
-                    c["sum"], w2_ref, c["i"], v_tall
-                )
+                mixed = c["lead"] * nn(c["x_wide"], tall(start)) + c["near"]
                 out_ref[c["sl"], h * width : (h + 1) * width] = mixed.astype(BF16)
 
     def arrived(piece):
@@ -441,11 +456,20 @@
     early = nz // 2
     for h in range(heads):
         prepare(h)
+    handed_in(0)
+
+    @pl.when(jnp.logical_not(at_once))
+    def _():
+        hand_in(1)
+
+    before = []
     for piece in range(2):
-        give_back(piece, row_prefix(piece))
-        hand_out(piece, 0, early)
+        before.append(row_prefix(piece))
+        give_back(piece)
+        hand_out(piece, before[piece], 0, early)
     for piece in range(2):
-        hand_out(piece, early, nz)
+        hand_out(piece, before[piece], early, nz)
+        trecv[piece, me_z] = tbuf[piece, me_z]
     arrived(0)
     runs = solve(range(heads))
     arrived(1)
@@ -453,6 +477,7 @@
     for piece in range(2):
         for d in range(1, nz):
             t_copy(piece, (me_z + d) % nz).wait_send()
+            s_copy(piece, d).wait_send()
         for y in range(1, ny):
 
             @pl.when(me_y < y)

time: 46.9 us -> 45.4 us (0.968)
  the two profiles are of different devices: /device:TPU:24 before, /device:TPU:25 now
where the time goes in v4:
time: 45.4 us; the launch traced here: 45.3 us
  Pallas kernels  43.6 us (96%)
  local copies, waits for them, and re-layouts  1.67 us (4%)
    pallas_call x1, Pallas kernels, body(): pl.pallas_call(functools.partial(kernel, ny, nz, nh), out_shape=jax.Shape...  43.6 us
    unnamed x1, local copies, waits for them, and re-layouts  1.67 us

profile of v4, /device:TPU:25, one launch (start us, length us, event | category | flops | bytes accessed | tf_op | source)
XLA Modules:
  0.0 45.3 jit_solution(13299325267167135369)
XLA Ops:
  0.0 43.6 %mesa.1 = bf16[512,256]{1,0:T(8,128)(2,1)} custom-call(bf16[512,256]{1,0:T(8,128)(2,1)} %feat_hbm.1, bf16[16,256]{1,0:T(8,128)(2,1)} %bitcast.2, bf16[512,256]{1,0:T(8,128)(2,1)} %q_hbm.1, bf16[512,256]{1,0:T(8,128)(2,1)} %k_hbm.1, bf16[512,256]{1,0:T(8,128)(2,1)} %v_hbm.1, f32[2,512]{1,0:T(2,128)} %bitcast.3, f32[2,128]{1,0:T(2,128)} %ridge_hbm.1), custom_call_target="tpu_custom_call" | custom-call | tf_op jit(solution)/shard_map/mesa/pallas_call | solution.py:497
  43.6 1.7 %copy.9 = bf16[512,256]{1,0:T(8,128)(2,1)} copy(bf16[512,256]{1,0:T(8,128)(2,1)} %mesa.1) | data formatting | bytes 524288

commit v5 on v4

--- a/solution.py
+++ b/solution.py
@@ -456,19 +456,23 @@
     early = nz // 2
     for h in range(heads):
         prepare(h)
-    handed_in(0)
+    close = [d for d in order if min(d, nz - d) <= 3]
+    for d in close:
+        s_copy(0, d).wait_recv()
 
     @pl.when(jnp.logical_not(at_once))
     def _():
         hand_in(1)
+
+    for d in order:
+        if d not in close:
+            s_copy(0, d).wait_recv()
 
     before = []
     for piece in range(2):
         before.append(row_prefix(piece))
         give_back(piece)
-        hand_out(piece, before[piece], 0, early)
-    for piece in range(2):
-        hand_out(piece, before[piece], early, nz)
+        hand_out(piece, before[piece], 0, nz)
         trecv[piece, me_z] = tbuf[piece, me_z]
     arrived(0)
     runs = solve(range(heads))

time: 45.4 us -> 44.3 us (0.976)
  the two profiles are of different devices: /device:TPU:25 before, /device:TPU:24 now
where the time goes in v5:
time: 44.3 us; the launch traced here: 44.1 us
  Pallas kernels  42.4 us (96%)
  local copies, waits for them, and re-layouts  1.67 us (4%)
    pallas_call x1, Pallas kernels, body(): pl.pallas_call(functools.partial(kernel, ny, nz, nh), out_shape=jax.Shape...  42.4 us
    unnamed x1, local copies, waits for them, and re-layouts  1.67 us

profile of v5, /device:TPU:24, one launch (start us, length us, event | category | flops | bytes accessed | tf_op | source)
XLA Modules:
  0.0 44.1 jit_solution(8980653355249647185)
XLA Ops:
  0.0 42.4 %mesa.1 = bf16[512,256]{1,0:T(8,128)(2,1)} custom-call(bf16[512,256]{1,0:T(8,128)(2,1)} %feat_hbm.1, bf16[16,256]{1,0:T(8,128)(2,1)} %bitcast.2, bf16[512,256]{1,0:T(8,128)(2,1)} %q_hbm.1, bf16[512,256]{1,0:T(8,128)(2,1)} %k_hbm.1, bf16[512,256]{1,0:T(8,128)(2,1)} %v_hbm.1, f32[2,512]{1,0:T(2,128)} %bitcast.3, f32[2,128]{1,0:T(2,128)} %ridge_hbm.1), custom_call_target="tpu_custom_call" | custom-call | tf_op jit(solution)/shard_map/mesa/pallas_call | solution.py:501
  42.4 1.7 %copy.9 = bf16[512,256]{1,0:T(8,128)(2,1)} copy(bf16[512,256]{1,0:T(8,128)(2,1)} %mesa.1) | data formatting | bytes 524288

commit v6 on v5

--- a/solution.py
+++ b/solution.py
@@ -241,9 +241,6 @@
 
     at_once = me_h % 2 == 0
 
-    @pl.when(at_once)
-    def _():
-        hand_in(1)
 
     lower = lax.broadcasted_iota(jnp.int32, (BLOCK, BLOCK), 0) >= lax.broadcasted_iota(
         jnp.int32, (BLOCK, BLOCK), 1
@@ -456,6 +453,10 @@
     early = nz // 2
     for h in range(heads):
         prepare(h)
+
+    @pl.when(at_once)
+    def _():
+        hand_in(1)
     close = [d for d in order if min(d, nz - d) <= 3]
     for d in close:
         s_copy(0, d).wait_recv()

time: 44.3 us -> 44.4 us (level)
  no operation moved by 1% of the time
where the time goes in v6:
time: 44.4 us; the launch traced here: 44.2 us
  Pallas kernels  42.5 us (96%)
  local copies, waits for them, and re-layouts  1.67 us (4%)
    pallas_call x1, Pallas kernels, body(): pl.pallas_call(functools.partial(kernel, ny, nz, nh), out_shape=jax.Shape...  42.5 us
    unnamed x1, local copies, waits for them, and re-layouts  1.67 us

profile of v6, /device:TPU:24, one launch (start us, length us, event | category | flops | bytes accessed | tf_op | source)
XLA Modules:
  0.0 44.2 jit_solution(1194642794410685569)
XLA Ops:
  0.0 42.5 %mesa.1 = bf16[512,256]{1,0:T(8,128)(2,1)} custom-call(bf16[512,256]{1,0:T(8,128)(2,1)} %feat_hbm.1, bf16[16,256]{1,0:T(8,128)(2,1)} %bitcast.2, bf16[512,256]{1,0:T(8,128)(2,1)} %q_hbm.1, bf16[512,256]{1,0:T(8,128)(2,1)} %k_hbm.1, bf16[512,256]{1,0:T(8,128)(2,1)} %v_hbm.1, f32[2,512]{1,0:T(2,128)} %bitcast.3, f32[2,128]{1,0:T(2,128)} %ridge_hbm.1), custom_call_target="tpu_custom_call" | custom-call | tf_op jit(solution)/shard_map/mesa/pallas_call | solution.py:502
  42.5 1.7 %copy.9 = bf16[512,256]{1,0:T(8,128)(2,1)} copy(bf16[512,256]{1,0:T(8,128)(2,1)} %mesa.1) | data formatting | bytes 524288
